TPU v7x, 32 devices: a whole 2x2x4 slice. The times are simulated.
32 devices in a mesh: row: 8 (over y, x, core), ka: 4 (over z).
Axes of the slice: x: 2, y: 2, z: 4, core: 2. Of those that a mesh axis runs over, the one named last changes fastest.
Arguments:
- pair_rep: bfloat16 [32, 32, 128], P('row', 'ka'), may hold values from -6 to 6
- in_weights: bfloat16 [2, 128, 512], replicated, may hold values from -0.5 to 0.5
- gate_weights: bfloat16 [2, 128, 128], replicated, may hold values from -0.5 to 0.5
- out_weights: bfloat16 [2, 128, 128], replicated, may hold values from -0.5 to 0.5
Outputs:
- refined: bfloat16 [32, 32, 128], P('row', 'ka')
All inputs are finite; a program needn't handle non-finite values.
Results may differ from a plain program's by a relative error of at most 0.015.
Values may be sent and summed in bfloat16 or wider, within the bound.
A program may use at most 64 MiB of HBM per device.

v0:
```python
import jax
import jax.numpy as jnp
from jax import lax
from jax.sharding import PartitionSpec as P

EPSILON = 1e-05


def normalize(values):
    values = values.astype(jnp.float32)
    centre = jnp.mean(values, axis=-1, keepdims=True)
    shifted = values - centre
    spread = jnp.mean(shifted * shifted, axis=-1, keepdims=True)
    return shifted * lax.rsqrt(spread + EPSILON)


def flatten_normed(blocks):
    normed = normalize(blocks).astype(jnp.bfloat16)
    return normed.reshape(-1, blocks.shape[-1])


def operands(flattened, weights, shape):
    columns = weights.shape[1] // 4
    projected = jnp.dot(flattened, weights, preferred_element_type=jnp.float32)
    left_rows = (
        jax.nn.sigmoid(projected[:, :columns]) * projected[:, columns : 2 * columns]
    ).astype(jnp.bfloat16)
    right_rows = (
        jax.nn.sigmoid(projected[:, 2 * columns : 3 * columns]) * projected[:, 3 * columns :]
    ).astype(jnp.bfloat16)
    return (
        left_rows.reshape(shape[0], shape[1], columns),
        right_rows.reshape(shape[0], shape[1], columns),
    )


def gates(flattened, weights, shape):
    gating = jax.nn.sigmoid(jnp.dot(flattened, weights, preferred_element_type=jnp.float32))
    return gating.reshape(shape[0], shape[1], weights.shape[1])


def triangle(left_rows, right_rows):
    partial_value = jnp.einsum(
        "ikh,jkh->ijh",
        left_rows,
        lax.all_gather(right_rows, "row", axis=0, tiled=True),
        preferred_element_type=jnp.float32,
    )
    return lax.psum_scatter(
        partial_value.astype(jnp.bfloat16), "ka", scatter_dimension=1, tiled=True
    ).astype(jnp.float32)


def finish(state, gating, product, weights):
    squeezed = normalize(product).astype(jnp.bfloat16).reshape(-1, product.shape[-1])
    update = jnp.dot(squeezed, weights, preferred_element_type=jnp.float32).reshape(gating.shape)
    return (state.astype(jnp.float32) + gating * update).astype(jnp.bfloat16)


def per_device(pair_rep, in_weights, gate_weights, out_weights):
    shape = pair_rep.shape
    flattened = flatten_normed(pair_rep)
    left_rows, right_rows = operands(flattened, in_weights[0], shape)
    gating = gates(flattened, gate_weights[0], shape)
    middle = finish(pair_rep, gating, triangle(left_rows, right_rows), out_weights[0])
    arrived = lax.all_to_all(
        jnp.swapaxes(middle, 0, 1), "ka", split_axis=1, concat_axis=0, tiled=True
    )
    arrived = lax.all_to_all(arrived, "row", split_axis=0, concat_axis=1, tiled=True)
    left_far, right_far = operands(flatten_normed(arrived), in_weights[1], arrived.shape)
    gating_far = gates(flatten_normed(middle), gate_weights[1], shape)
    return finish(middle, gating_far, triangle(left_far, right_far), out_weights[1])


def solution(mesh):
    in_specs = (P("row", "ka", None), P(), P(), P())
    out_specs = P("row", "ka", None)
    return jax.shard_map(
        per_device, mesh=mesh, in_specs=in_specs, out_specs=out_specs, check_vma=False
    )
```

profile of v0, /device:TPU:0, one launch (start us, length us, event | category | flops | bytes accessed | tf_op | source)
XLA Modules:
  0.0 86.3 jit_solution(1620669610929316636)
XLA Ops:
  0.0 0.9 convert_reduce_fusion.1
  1.0 1.1 %fusion.16 = f32[32,512]{1,0:T(8,128)S(1)} fusion(bf16[2,128,512]{2,1,0:T(8,128)(2,1)} %param.5, bf16[4,8,128]{2,1,0:T(8,128)(2,1)S(1)} %copy-done.1, f32[4,8]{1,0:T(4,128)S(1)} %add_rsqrt_fusion.4, f32[4,8]{1,0:T(4,128)S(1)} %broadcast_multiply_fusion.4), kind=kOutput, calls=%fused_computation.22 | convolution fusion | flops 4210688 | bytes 205056 | tf_op jit(solution)/shard_map/dot_general | solution.py:24
  2.2 10.7 %all_gather.6 = bf16[32,8,128]{2,1,0:T(8,128)(2,1)S(1)} all-gather(bf16[4,8,128]{2,1,0:T(8,128)(2,1)S(1)} %get-tuple-element.8), channel_id=1, replica_groups=mesh['row'=8,'ka'=4] {'row'}, dimensions={0}, use_global_device_ids=true | all-gather | bytes 73728 | tf_op jit(solution)/shard_map/all_gather | solution.py:46
  12.9 1.4 %copy.65 = bf16[32,8,128]{1,0,2:T(8,128)(2,1)S(1)} copy(bf16[32,8,128]{2,1,0:T(8,128)(2,1)S(1)} %all_gather.6) | data formatting | bytes 131072 | tf_op jit(solution)/shard_map/all_gather | solution.py:46
  14.5 0.6 fusion
  15.3 19.4 %all-reduce = bf16[4,32,128]{2,0,1:T(4,128)(2,1)S(1)} all-reduce(bf16[4,32,128]{2,0,1:T(4,128)(2,1)S(1)} %copy.67), channel_id=2, replica_groups=mesh['row'=8,'ka'=4] {'ka'}, use_global_device_ids=true, to_apply=%region_2.0.clone | all-reduce | flops 16384 | bytes 65536
  34.7 0.6 copy-done.4
  35.3 0.6 dynamic-slice
  37.2 0.4 copy-done.2
  37.5 0.7 convert_reduce_fusion
  38.3 3.2 %all-to-all-start = ((bf16[8,4,128]{2,0,1:T(8,128)(2,1)}), bf16[8,4,128]{2,0,1:T(8,128)(2,1)S(1)}, u32[]{:S(2)}, u32[]{:S(2)}) async-start(bf16[8,4,128]{2,0,1:T(8,128)(2,1)} %bitcast.12), calls=%async_computation | async-start | bytes 16384 | tf_op jit(solution)/shard_map/all_to_all | solution.py:66
  41.5 0.9 %fusion.42 = f32[4,8]{1,0:T(4,128)S(1)} fusion(bf16[4,8,128]{2,1,0:T(8,128)(2,1)} %get-tuple-element.10, f32[4,8]{1,0:T(4,128)S(1)} %broadcast_multiply_fusion.3), kind=kLoop, calls=%fused_computation.58 | loop fusion | flops 16352 | bytes 8448 | tf_op jit(solution)/shard_map/reduce_sum | solution.py:13
  42.4 4.6 %all-to-all-done = bf16[8,4,128]{2,0,1:T(8,128)(2,1)S(1)} async-done(((bf16[8,4,128]{2,0,1:T(8,128)(2,1)}), bf16[8,4,128]{2,0,1:T(8,128)(2,1)S(1)}, u32[]{:S(2)}, u32[]{:S(2)}) %all-to-all-start) | async-done | bytes 8224 | tf_op jit(solution)/shard_map/all_to_all | solution.py:66
  47.1 0.6 broadcast.145
  47.7 0.7 reduce.1
  48.4 0.6 reshape.129
  49.0 3.3 %all-to-all-start.1 = ((bf16[8,2,256]{2,1,0:T(2,128)(2,1)}), bf16[8,2,256]{2,1,0:T(2,128)(2,1)S(1)}, u32[]{:S(2)}, u32[]{:S(2)}) async-start(bf16[8,2,256]{2,1,0:T(2,128)(2,1)} %reshape.129), calls=%async_computation.1 | async-start | bytes 16384 | tf_op jit(solution)/shard_map/all_to_all | solution.py:69
  52.3 0.9 %fusion.6 = f32[4,8,128]{2,1,0:T(8,128)S(1)} fusion(bf16[2,128,128]{2,1,0:T(8,128)(2,1)S(1)} %copy-done.3, bf16[4,8,128]{2,1,0:T(8,128)(2,1)} %get-tuple-element.10, f32[4,8]{1,0:T(4,128)S(1)} %add_rsqrt_fusion.3, f32[4,8]{1,0:T(4,128)S(1)} %broadcast_multiply_fusion.3), kind=kOutput, calls=%fused_computation.10 | convolution fusion | flops 1077248 | bytes 61440 | tf_op jit(solution)/shard_map/dot_general | solution.py:38
  53.2 3.7 %all-to-all-done.1 = bf16[8,2,256]{2,1,0:T(2,128)(2,1)S(1)} async-done(((bf16[8,2,256]{2,1,0:T(2,128)(2,1)}), bf16[8,2,256]{2,1,0:T(2,128)(2,1)S(1)}, u32[]{:S(2)}, u32[]{:S(2)}) %all-to-all-start.1) | async-done | bytes 8224 | tf_op jit(solution)/shard_map/all_to_all | solution.py:69
  57.5 8.3 %all_gather.7 = bf16[32,8,128]{2,1,0:T(8,128)(2,1)S(1)} all-gather(bf16[4,8,128]{2,1,0:T(8,128)(2,1)S(1)} %get-tuple-element.6), channel_id=1, replica_groups=mesh['row'=8,'ka'=4] {'row'}, dimensions={0}, use_global_device_ids=true | all-gather | bytes 73728 | tf_op jit(solution)/shard_map/all_gather | solution.py:46
  65.8 1.4 %copy.81 = bf16[32,8,128]{1,0,2:T(8,128)(2,1)S(1)} copy(bf16[32,8,128]{2,1,0:T(8,128)(2,1)S(1)} %all_gather.7) | data formatting | bytes 131072 | tf_op jit(solution)/shard_map/all_gather | solution.py:46
  67.4 0.6 fusion.1
  68.2 16.3 %all-reduce.1 = bf16[4,32,128]{2,0,1:T(4,128)(2,1)S(1)} all-reduce(bf16[4,32,128]{2,0,1:T(4,128)(2,1)S(1)} %copy.83), channel_id=3, replica_groups=mesh['row'=8,'ka'=4] {'ka'}, use_global_device_ids=true, to_apply=%region_9.0.clone | all-reduce | flops 16384 | bytes 65536
  84.8 1.4 %fusion.13 = bf16[4,8,128]{2,1,0:T(8,128)(2,1)} fusion(f32[4,8,128]{2,1,0:T(8,128)S(1)} %fusion.6, bf16[2,128,128]{2,1,0:T(8,128)(2,1)S(1)} %copy-done.2, bf16[4,8,128]{2,1,0:T(8,128)(2,1)} %get-tuple-element.10, bf16[4,8,128]{2,0,1:T(4,128)(2,1)S(1)} %fusion.39), kind=kOutput, calls=%fused_computation.19 | convolution fusion | flops 1064960 | bytes 73728 | tf_op jit(solution)/shard_map/dot_general | solution.py:56
  (38 shorter events, 2.2 us)
Async XLA Ops:
  0.0 0.9 %copy-start.1 = (bf16[4,8,128]{2,1,0:T(8,128)(2,1)S(1)}, bf16[4,8,128]{2,1,0:T(8,128)(2,1)}, u32[]{:S(2)}) copy-start(bf16[4,8,128]{2,1,0:T(8,128)(2,1)} %param.4) | copy-start | bytes 24580
  15.3 21.7 %copy-start.3 = (bf16[2,128,128]{2,1,0:T(8,128)(2,1)S(1)}, bf16[2,128,128]{2,1,0:T(8,128)(2,1)}, u32[]{:S(2)}) copy-start(bf16[2,128,128]{2,1,0:T(8,128)(2,1)} %param.6) | copy-start | bytes 196612
  34.7 0.7 copy-start.4
  36.7 0.8 copy-start.2
  37.0 20.4 %copy-start = (bf16[2,128,512]{2,1,0:T(8,128)(2,1)S(1)}, bf16[2,128,512]{2,1,0:T(8,128)(2,1)}, u32[]{:S(2)}) copy-start(bf16[2,128,512]{2,1,0:T(8,128)(2,1)} %param.5) | copy-start | bytes 786436
  38.3 8.8 %all-to-all-start = ((bf16[8,4,128]{2,0,1:T(8,128)(2,1)}), bf16[8,4,128]{2,0,1:T(8,128)(2,1)S(1)}, u32[]{:S(2)}, u32[]{:S(2)}) async-start(bf16[8,4,128]{2,0,1:T(8,128)(2,1)} %bitcast.12), calls=%async_computation | async-start | bytes 16384 | tf_op jit(solution)/shard_map/all_to_all | solution.py:66
  49.0 8.0 %all-to-all-start.1 = ((bf16[8,2,256]{2,1,0:T(2,128)(2,1)}), bf16[8,2,256]{2,1,0:T(2,128)(2,1)S(1)}, u32[]{:S(2)}, u32[]{:S(2)}) async-start(bf16[8,2,256]{2,1,0:T(2,128)(2,1)} %reshape.129), calls=%async_computation.1 | async-start | bytes 16384 | tf_op jit(solution)/shard_map/all_to_all | solution.py:69
where the time goes:
time: 86.9 us; the launch traced here: 86.3 us
  blocking collectives  54.7 us (63%)
  waiting for transfers between devices  8.39 us (10%)
  starting transfers between devices  6.58 us (8%)
  local copies, waits for them, and re-layouts  6.25 us (7%)
  matrix products  5.78 us (7%)
  other arithmetic  3.7 us (4%)
  between operations  0.88 us (1%)
    unnamed x2, blocking collectives  35.7 us
    all_gather x2, blocking collectives, triangle(): lax.all_gather(right_rows, 'row', axis=0, tiled=True)  19 us
    all_to_all x1, waiting for transfers between devices, per_device(): lax.all_to_all(jnp.swapaxes(middle, 0, 1), 'ka', split_axis=1, concat_axi...  4.65 us
    all_to_all x1, waiting for transfers between devices, per_device(): lax.all_to_all(arrived, 'row', split_axis=0, concat_axis=1, tiled=True)  3.74 us
    all_to_all x1, starting transfers between devices, per_device(): lax.all_to_all(arrived, 'row', split_axis=0, concat_axis=1, tiled=True)  3.33 us
    all_to_all x1, starting transfers between devices, per_device(): lax.all_to_all(jnp.swapaxes(middle, 0, 1), 'ka', split_axis=1, concat_axi...  3.25 us
    all_gather x2, local copies, waits for them, and re-layouts, triangle(): lax.all_gather(right_rows, 'row', axis=0, tiled=True)  2.86 us
    unnamed x13, local copies, waits for them, and re-layouts  2.22 us
  transfers between devices with their start and end apart: 2, of which 2 were waited for; matrix products, arithmetic and copies ran while one was open for 2% of the time, Pallas kernels for 0%

commit v1 on v0

--- a/solution.py
+++ b/solution.py
@@ -1,9 +1,15 @@
+import functools
+
 import jax
 import jax.numpy as jnp
 from jax import lax
+from jax.experimental import pallas as pl
+from jax.experimental.pallas import tpu as pltpu
 from jax.sharding import PartitionSpec as P
 
 EPSILON = 1e-05
+MESH = pl.DeviceIdType.MESH
+VMEM_BUDGET = 32 * 1024 * 1024
 
 
 def normalize(values):
@@ -57,7 +63,7 @@
     return (state.astype(jnp.float32) + gating * update).astype(jnp.bfloat16)
 
 
-def per_device(pair_rep, in_weights, gate_weights, out_weights):
+def per_device_large(pair_rep, in_weights, gate_weights, out_weights):
     shape = pair_rep.shape
     flattened = flatten_normed(pair_rep)
     left_rows, right_rows = operands(flattened, in_weights[0], shape)
@@ -72,9 +78,195 @@
     return finish(middle, gating_far, triangle(left_far, right_far), out_weights[1])
 
 
+def gated(normed, weights):
+    half = weights.shape[1] // 2
+    projected = jnp.dot(normed, weights, preferred_element_type=jnp.float32)
+    rounded = (jax.nn.sigmoid(projected[:, :half]) * projected[:, half:]).astype(jnp.bfloat16)
+    return rounded.astype(jnp.float32)
+
+
+def closing(state, normed, product, gate_w, out_w):
+    update = jnp.dot(
+        normalize(product).astype(jnp.bfloat16), out_w, preferred_element_type=jnp.float32
+    )
+    gating = jax.nn.sigmoid(jnp.dot(normed, gate_w, preferred_element_type=jnp.float32))
+    return (state.astype(jnp.float32) + gating * update).astype(jnp.bfloat16)
+
+
+def gather_blocks(R, K, x_ref, full, own_sem, send_sem, recv_sem, fsend_sem, frecv_sem):
+    r, c = lax.axis_index("row"), lax.axis_index("ka")
+    partner = r + 1 - 2 * lax.rem(r, 2)
+    offsets = [(dr, dc) for dr in range(R // 2) for dc in range(K)][1:]
+    own = pltpu.make_async_copy(x_ref, full.at[r, c], own_sem)
+    own.start()
+
+    def away(dr, dc):
+        return lax.rem(r + 2 * dr, R), lax.rem(c + dc, K)
+
+    def back(row, dr, dc):
+        return lax.rem(row + R - 2 * dr, R), lax.rem(c + K - dc, K)
+
+    barrier = pltpu.get_barrier_semaphore()
+    for dr, dc in offsets:
+        pl.semaphore_signal(barrier, inc=1, device_id=away(dr, dc), device_id_type=MESH)
+    pl.semaphore_signal(barrier, inc=1, device_id=(partner, c), device_id_type=MESH)
+    own.wait()
+    pl.semaphore_wait(barrier, len(offsets) + 1)
+
+    def direct(dr, dc, block):
+        at = dr * K + dc
+        return pltpu.make_async_remote_copy(
+            src_ref=full.at[block], dst_ref=full.at[block],
+            send_sem=send_sem.at[at], recv_sem=recv_sem.at[at],
+            device_id=away(dr, dc), device_id_type=MESH,
+        )
+
+    def forward(dr, dc, block):
+        at = dr * K + dc
+        return pltpu.make_async_remote_copy(
+            src_ref=full.at[block], dst_ref=full.at[block],
+            send_sem=fsend_sem.at[at], recv_sem=frecv_sem.at[at],
+            device_id=(partner, c), device_id_type=MESH,
+        )
+
+    sent = [direct(dr, dc, (r, c)) for dr, dc in reversed(offsets)]
+    for copy in sent:
+        copy.start()
+    forwards = [forward(0, 0, (r, c))]
+    forwards[0].start()
+    for dr, dc in offsets:
+        block = back(r, dr, dc)
+        direct(dr, dc, block).wait_recv()
+        copy = forward(dr, dc, block)
+        copy.start()
+        forwards.append(copy)
+    for dr, dc in [(0, 0)] + offsets:
+        forward(dr, dc, back(partner, dr, dc)).wait_recv()
+    for copy in sent + forwards:
+        copy.wait_send()
+
+
+def kernel(
+    R, K, rows, cols,
+    x_ref, iw_hbm, gw_hbm, ow_hbm, o_ref,
+    full, iw, gw, ow, norm, left, right, tri, mid, norm1, left1,
+    own_sem, w_sem, send_sem, recv_sem, fsend_sem, frecv_sem,
+):
+    r, c = lax.axis_index("row"), lax.axis_index("ka")
+    loads = [
+        pltpu.make_async_copy(src, dst, w_sem.at[n])
+        for n, (src, dst) in enumerate(((iw_hbm, iw), (gw_hbm, gw), (ow_hbm, ow)))
+    ]
+    for load in loads:
+        load.start()
+    gather_blocks(R, K, x_ref, full, own_sem, send_sem, recv_sem, fsend_sem, frecv_sem)
+    for load in loads:
+        load.wait()
+    compute(R, K, rows, cols, r, c, o_ref, full, iw, gw, ow, norm, left, right, tri, mid, norm1, left1)
+
+
+def compute(R, K, rows, cols, r, c, o_ref, full, iw, gw, ow, norm, left, right, tri, mid, norm1, left1):
+    ch = o_ref.shape[-1]
+    hidden = ow.shape[1]
+    span = cols // rows
+    size = rows * cols
+    groups = (c, r // span)
+
+    def project(rb, carry):
+        normed = normalize(full[rb].reshape(K * size, ch)).astype(jnp.bfloat16)
+        norm[rb] = normed.reshape(K, size, ch)
+        left[rb] = gated(normed, iw[0, :, : 2 * hidden]).reshape(K, rows, cols, hidden)
+        return carry
+
+    lax.fori_loop(0, R, project, 0)
+    for g, block in enumerate(groups):
+        for part in range(span):
+            values = gated(norm[block * span + part].reshape(K * size, ch), iw[0, :, 2 * hidden :])
+            for k in range(K):
+                at = ((g * K + k) * span + part) * size
+                right[at : at + size, :] = values[k * size : (k + 1) * size]
+
+    def outgoing(rb, carry):
+        totals = [jnp.zeros((rows, cols, hidden), jnp.float32) for _ in groups]
+        for k in range(K):
+            for b in range(cols):
+                row = left[rb, k, :, b : b + 1, :]
+                for g in range(2):
+                    other = right[pl.ds((g * K + k) * span * size + b, cols, stride=cols), :]
+                    totals[g] = totals[g] + row * other[None]
+        for g in range(2):
+            tri[g, rb] = totals[g].reshape(size, hidden)
+        return carry
+
+    lax.fori_loop(0, R, outgoing, 0)
+    for g, block in enumerate(groups):
+        state = full[:, block].reshape(R * size, ch)
+        normed = norm[:, block].reshape(R * size, ch)
+        product = tri[g].reshape(R * size, hidden)
+        middle = closing(state, normed, product, gw[0], ow[0])
+        again = normalize(middle).astype(jnp.bfloat16)
+        if g == 0:
+            mid[...] = middle.reshape(R, size, ch)
+            norm1[...] = again.reshape(R, size, ch)
+            right1 = gated(again, iw[1, :, 2 * hidden :]).reshape(R * rows, cols, hidden)
+            right[: R * size, :] = right1.reshape(R * size, hidden)
+        else:
+            left1[...] = gated(again, iw[1, :, : 2 * hidden])
+    first = lax.rem(r, span) * rows
+    totals = [jnp.zeros((cols, hidden), jnp.float32) for _ in range(rows)]
+    for k in range(R * rows):
+        other = right[k * cols : (k + 1) * cols, :]
+        for a in range(rows):
+            totals[a] = totals[a] + left1[pl.ds(k * cols + first + a, 1), :] * other
+    product = jnp.concatenate(totals, axis=0)
+    o_ref[...] = closing(mid[r], norm1[r], product, gw[1], ow[1])
+
+
+def per_device(R, K, pair_rep, in_weights, gate_weights, out_weights):
+    rows, cols, ch = pair_rep.shape
+    hidden = out_weights.shape[1]
+    size = rows * cols
+    span = cols // rows
+    scratch = [
+        pltpu.VMEM((R, K, size, ch), jnp.bfloat16),
+        pltpu.VMEM(in_weights.shape, jnp.bfloat16),
+        pltpu.VMEM(gate_weights.shape, jnp.bfloat16),
+        pltpu.VMEM(out_weights.shape, jnp.bfloat16),
+        pltpu.VMEM((R, K, size, ch), jnp.bfloat16),
+        pltpu.VMEM((R, K, rows, cols, hidden), jnp.float32),
+        pltpu.VMEM((2 * K * span * size, hidden), jnp.float32),
+        pltpu.VMEM((2, R, size, hidden), jnp.float32),
+        pltpu.VMEM((R, size, ch), jnp.bfloat16),
+        pltpu.VMEM((R, size, ch), jnp.bfloat16),
+        pltpu.VMEM((R * size, hidden), jnp.float32),
+        pltpu.SemaphoreType.DMA,
+        pltpu.SemaphoreType.DMA((3,)),
+    ] + [pltpu.SemaphoreType.DMA((R // 2 * K,))] * 4
+    result = pl.pallas_call(
+        functools.partial(kernel, R, K, rows, cols),
+        out_shape=jax.ShapeDtypeStruct((size, ch), jnp.bfloat16),
+        in_specs=[pl.BlockSpec(memory_space=pl.ANY)] * 4,
+        out_specs=pl.BlockSpec(memory_space=pltpu.VMEM),
+        scratch_shapes=scratch,
+        compiler_params=pltpu.CompilerParams(collective_id=0, has_side_effects=True),
+    )(pair_rep.reshape(size, ch), in_weights, gate_weights, out_weights)
+    return result.reshape(rows, cols, ch)
+
+
 def solution(mesh):
+    R, K = mesh.shape["row"], mesh.shape["ka"]
+
+    def body(pair_rep, in_weights, gate_weights, out_weights):
+        rows, cols, ch = pair_rep.shape
+        bytes_held = 8 * R * K * rows * cols * max(ch, out_weights.shape[1])
+        small = bytes_held < VMEM_BUDGET and R % 2 == 0 and cols % rows == 0
+        whole = R * rows == K * cols and cols % 8 == 0
+        if small and whole:
+            return per_device(R, K, pair_rep, in_weights, gate_weights, out_weights)
+        return per_device_large(pair_rep, in_weights, gate_weights, out_weights)
+
     in_specs = (P("row", "ka", None), P(), P(), P())
     out_specs = P("row", "ka", None)
     return jax.shard_map(
-        per_device, mesh=mesh, in_specs=in_specs, out_specs=out_specs, check_vma=False
-    )
+        body, mesh=mesh, in_specs=in_specs, out_specs=out_specs, check_vma=False
+    )

time: 86.9 us -> 19.7 us (0.23)
  the two profiles are of different devices: /device:TPU:0 before, /device:TPU:1 now
where the time goes in v1:
time: 19.7 us; the launch traced here: 19.3 us
  Pallas kernels  18 us (91%)
  local copies, waits for them, and re-layouts  1.3 us (7%)
    pallas_call x1, Pallas kernels, per_device(): pl.pallas_call(functools.partial(kernel, R, K, rows, cols), out_shape=jax...  18 us
    unnamed x1, local copies, waits for them, and re-layouts  1.3 us

profile of v1, /device:TPU:1, one launch (start us, length us, event | category | flops | bytes accessed | tf_op | source)
XLA Modules:
  0.0 19.3 jit_solution(10052653148472414276)
XLA Ops:
  0.0 18.0 %shard_map.46 = bf16[32,128]{1,0:T(8,128)(2,1)} custom-call(bf16[32,128]{1,0:T(8,128)(2,1)} %bitcast.3, bf16[2,128,512]{2,1,0:T(8,128)(2,1)} %iw_hbm.1, bf16[2,128,128]{2,1,0:T(8,128)(2,1)} %gw_hbm.1, bf16[2,128,128]{2,1,0:T(8,128)(2,1)} %ow_hbm.1), custom_call_target="tpu_custom_call" | custom-call | tf_op jit(solution)/shard_map/pallas_call | solution.py:245
  18.0 1.3 %copy.6 = bf16[4,8,128]{2,1,0:T(8,128)(2,1)} copy(bf16[4,8,128]{2,1,0:T(8,128)(2,1)} %bitcast.2) | data formatting | bytes 16384

commit v2 on v1

--- a/solution.py
+++ b/solution.py
@@ -93,92 +93,88 @@
     return (state.astype(jnp.float32) + gating * update).astype(jnp.bfloat16)
 
 
-def gather_blocks(R, K, x_ref, full, own_sem, send_sem, recv_sem, fsend_sem, frecv_sem):
-    r, c = lax.axis_index("row"), lax.axis_index("ka")
-    partner = r + 1 - 2 * lax.rem(r, 2)
-    offsets = [(dr, dc) for dr in range(R // 2) for dc in range(K)][1:]
-    own = pltpu.make_async_copy(x_ref, full.at[r, c], own_sem)
-    own.start()
-
-    def away(dr, dc):
-        return lax.rem(r + 2 * dr, R), lax.rem(c + dc, K)
-
-    def back(row, dr, dc):
-        return lax.rem(row + R - 2 * dr, R), lax.rem(c + K - dc, K)
-
-    barrier = pltpu.get_barrier_semaphore()
-    for dr, dc in offsets:
-        pl.semaphore_signal(barrier, inc=1, device_id=away(dr, dc), device_id_type=MESH)
-    pl.semaphore_signal(barrier, inc=1, device_id=(partner, c), device_id_type=MESH)
-    own.wait()
-    pl.semaphore_wait(barrier, len(offsets) + 1)
-
-    def direct(dr, dc, block):
-        at = dr * K + dc
-        return pltpu.make_async_remote_copy(
-            src_ref=full.at[block], dst_ref=full.at[block],
-            send_sem=send_sem.at[at], recv_sem=recv_sem.at[at],
-            device_id=away(dr, dc), device_id_type=MESH,
-        )
-
-    def forward(dr, dc, block):
-        at = dr * K + dc
-        return pltpu.make_async_remote_copy(
-            src_ref=full.at[block], dst_ref=full.at[block],
-            send_sem=fsend_sem.at[at], recv_sem=frecv_sem.at[at],
-            device_id=(partner, c), device_id_type=MESH,
-        )
-
-    sent = [direct(dr, dc, (r, c)) for dr, dc in reversed(offsets)]
-    for copy in sent:
-        copy.start()
-    forwards = [forward(0, 0, (r, c))]
-    forwards[0].start()
-    for dr, dc in offsets:
-        block = back(r, dr, dc)
-        direct(dr, dc, block).wait_recv()
-        copy = forward(dr, dc, block)
-        copy.start()
-        forwards.append(copy)
-    for dr, dc in [(0, 0)] + offsets:
-        forward(dr, dc, back(partner, dr, dc)).wait_recv()
-    for copy in sent + forwards:
-        copy.wait_send()
-
-
 def kernel(
     R, K, rows, cols,
     x_ref, iw_hbm, gw_hbm, ow_hbm, o_ref,
-    full, iw, gw, ow, norm, left, right, tri, mid, norm1, left1,
-    own_sem, w_sem, send_sem, recv_sem, fsend_sem, frecv_sem,
+    full, iw, gw, ow, norm, left, right, turned, tri, mid, norm1, left1,
+    own_sem, w_sem, dsend, drecv, fsend, frecv,
 ):
     r, c = lax.axis_index("row"), lax.axis_index("ka")
+    partner = r + 1 - 2 * lax.rem(r, 2)
+    H = R // 2
+    own = pltpu.make_async_copy(x_ref, full.at[r, c], own_sem)
+    own.start()
     loads = [
         pltpu.make_async_copy(src, dst, w_sem.at[n])
         for n, (src, dst) in enumerate(((iw_hbm, iw), (gw_hbm, gw), (ow_hbm, ow)))
     ]
     for load in loads:
         load.start()
-    gather_blocks(R, K, x_ref, full, own_sem, send_sem, recv_sem, fsend_sem, frecv_sem)
+
+    def ahead(dr, dc):
+        return lax.rem(r + 2 * dr, R), lax.rem(c + dc, K)
+
+    def behind(row, dr, dc):
+        return lax.rem(row + R - 2 * dr, R), lax.rem(c + K - dc, K)
+
+    barrier = pltpu.get_barrier_semaphore()
+    offsets = [(dr, dc) for dr in range(H) for dc in range(K)]
+    for dr, dc in offsets[1:]:
+        pl.semaphore_signal(barrier, inc=1, device_id=ahead(dr, dc), device_id_type=MESH)
+    pl.semaphore_signal(barrier, inc=1, device_id=(partner, c), device_id_type=MESH)
+    own.wait()
+    pl.semaphore_wait(barrier, len(offsets))
+
+    def remote(block, device, send, recv):
+        return pltpu.make_async_remote_copy(
+            src_ref=full.at[block], dst_ref=full.at[block], send_sem=send, recv_sem=recv,
+            device_id=device, device_id_type=MESH,
+        )
+
+    def direct(dr, dc, block):
+        return remote(block, ahead(dr, dc), dsend.at[dr, dc], drecv.at[dr, dc])
+
+    def to_partner(dr, dc, block):
+        return remote(block, (partner, c), fsend.at[dr, dc], frecv.at[dr, dc])
+
+    sent = []
+
+    def start(copy):
+        copy.start()
+        sent.append(copy)
+
+    def project(rb):
+        normed = normalize(full[rb].reshape(K * rows * cols, full.shape[-1])).astype(jnp.bfloat16)
+        norm[rb] = normed.reshape(norm.shape[1:])
+        left[rb] = gated(normed, iw[0, :, : 2 * ow.shape[1]]).reshape(left.shape[1:])
+
+    for dr, dc in offsets[1:]:
+        start(direct(dr, dc, (r, c)))
+    start(to_partner(0, 0, (r, c)))
     for load in loads:
         load.wait()
-    compute(R, K, rows, cols, r, c, o_ref, full, iw, gw, ow, norm, left, right, tri, mid, norm1, left1)
-
-
-def compute(R, K, rows, cols, r, c, o_ref, full, iw, gw, ow, norm, left, right, tri, mid, norm1, left1):
+    for dr, dc in offsets[1:]:
+        block = behind(r, dr, dc)
+        direct(dr, dc, block).wait_recv()
+        start(to_partner(dr, dc, block))
+    for dr in range(H):
+        project(behind(r, dr, 0)[0])
+    for dr, dc in offsets:
+        to_partner(dr, dc, behind(partner, dr, dc)).wait_recv()
+    for dr in range(H):
+        project(behind(partner, dr, 0)[0])
+    for copy in sent:
+        copy.wait_send()
+    compute(R, K, rows, cols, r, c, o_ref, full, iw, gw, ow, norm, left, right, turned, tri, mid, norm1, left1)
+
+
+def compute(R, K, rows, cols, r, c, o_ref, full, iw, gw, ow, norm, left, right, turned, tri, mid, norm1, left1):
     ch = o_ref.shape[-1]
     hidden = ow.shape[1]
     span = cols // rows
     size = rows * cols
     groups = (c, r // span)
 
-    def project(rb, carry):
-        normed = normalize(full[rb].reshape(K * size, ch)).astype(jnp.bfloat16)
-        norm[rb] = normed.reshape(K, size, ch)
-        left[rb] = gated(normed, iw[0, :, : 2 * hidden]).reshape(K, rows, cols, hidden)
-        return carry
-
-    lax.fori_loop(0, R, project, 0)
     for g, block in enumerate(groups):
         for part in range(span):
             values = gated(norm[block * span + part].reshape(K * size, ch), iw[0, :, 2 * hidden :])
@@ -186,19 +182,24 @@
                 at = ((g * K + k) * span + part) * size
                 right[at : at + size, :] = values[k * size : (k + 1) * size]
 
+    for g in range(2):
+        for k in range(K):
+            for b in range(cols):
+                at = (g * K + k) * span * size + b
+                turned[g, k * cols + b] = right[pl.ds(at, cols, stride=cols), :]
+
     def outgoing(rb, carry):
         totals = [jnp.zeros((rows, cols, hidden), jnp.float32) for _ in groups]
         for k in range(K):
             for b in range(cols):
                 row = left[rb, k, :, b : b + 1, :]
                 for g in range(2):
-                    other = right[pl.ds((g * K + k) * span * size + b, cols, stride=cols), :]
-                    totals[g] = totals[g] + row * other[None]
+                    totals[g] = totals[g] + row * turned[g, k * cols + b][None]
         for g in range(2):
             tri[g, rb] = totals[g].reshape(size, hidden)
         return carry
 
-    lax.fori_loop(0, R, outgoing, 0)
+    lax.fori_loop(0, R, outgoing, 0, unroll=2)
     for g, block in enumerate(groups):
         state = full[:, block].reshape(R * size, ch)
         normed = norm[:, block].reshape(R * size, ch)
@@ -235,13 +236,14 @@
         pltpu.VMEM((R, K, size, ch), jnp.bfloat16),
         pltpu.VMEM((R, K, rows, cols, hidden), jnp.float32),
         pltpu.VMEM((2 * K * span * size, hidden), jnp.float32),
+        pltpu.VMEM((2, K * cols, cols, hidden), jnp.float32),
         pltpu.VMEM((2, R, size, hidden), jnp.float32),
         pltpu.VMEM((R, size, ch), jnp.bfloat16),
         pltpu.VMEM((R, size, ch), jnp.bfloat16),
         pltpu.VMEM((R * size, hidden), jnp.float32),
         pltpu.SemaphoreType.DMA,
         pltpu.SemaphoreType.DMA((3,)),
-    ] + [pltpu.SemaphoreType.DMA((R // 2 * K,))] * 4
+    ] + [pltpu.SemaphoreType.DMA((R // 2, K))] * 4
     result = pl.pallas_call(
         functools.partial(kernel, R, K, rows, cols),
         out_shape=jax.ShapeDtypeStruct((size, ch), jnp.bfloat16),

time: 19.7 us -> 16.9 us (0.86)
  Pallas kernels: 18 us -> 15.4 us
    pallas_call x1, Pallas kernels: 18 us -> 15.4 us  [per_device(): pl.pallas_call(functools.partial(kernel, R, K, rows, cols), out_shape=jax...]
where the time goes in v2:
time: 16.9 us; the launch traced here: 16.7 us
  Pallas kernels  15.4 us (91%)
  local copies, waits for them, and re-layouts  1.3 us (8%)
    pallas_call x1, Pallas kernels, per_device(): pl.pallas_call(functools.partial(kernel, R, K, rows, cols), out_shape=jax...  15.4 us
    unnamed x1, local copies, waits for them, and re-layouts  1.3 us

profile of v2, /device:TPU:1, one launch (start us, length us, event | category | flops | bytes accessed | tf_op | source)
XLA Modules:
  0.0 16.7 jit_solution(5727667131684457816)
XLA Ops:
  0.0 15.4 %shard_map.46 = bf16[32,128]{1,0:T(8,128)(2,1)} custom-call(bf16[32,128]{1,0:T(8,128)(2,1)} %bitcast.3, bf16[2,128,512]{2,1,0:T(8,128)(2,1)} %iw_hbm.1, bf16[2,128,128]{2,1,0:T(8,128)(2,1)} %gw_hbm.1, bf16[2,128,128]{2,1,0:T(8,128)(2,1)} %ow_hbm.1), custom_call_target="tpu_custom_call" | custom-call | tf_op jit(solution)/shard_map/pallas_call | solution.py:247
  15.4 1.3 %copy.6 = bf16[4,8,128]{2,1,0:T(8,128)(2,1)} copy(bf16[4,8,128]{2,1,0:T(8,128)(2,1)} %bitcast.2) | data formatting | bytes 16384

commit v3 on v2

--- a/solution.py
+++ b/solution.py
@@ -163,9 +163,9 @@
         to_partner(dr, dc, behind(partner, dr, dc)).wait_recv()
     for dr in range(H):
         project(behind(partner, dr, 0)[0])
+    compute(R, K, rows, cols, r, c, o_ref, full, iw, gw, ow, norm, left, right, turned, tri, mid, norm1, left1)
     for copy in sent:
         copy.wait_send()
-    compute(R, K, rows, cols, r, c, o_ref, full, iw, gw, ow, norm, left, right, turned, tri, mid, norm1, left1)
 
 
 def compute(R, K, rows, cols, r, c, o_ref, full, iw, gw, ow, norm, left, right, turned, tri, mid, norm1, left1):
@@ -250,7 +250,7 @@
         in_specs=[pl.BlockSpec(memory_space=pl.ANY)] * 4,
         out_specs=pl.BlockSpec(memory_space=pltpu.VMEM),
         scratch_shapes=scratch,
-        compiler_params=pltpu.CompilerParams(collective_id=0, has_side_effects=True),
+        compiler_params=pltpu.CompilerParams(collective_id=0, has_side_effects=True, vmem_limit_bytes=56542968),
     )(pair_rep.reshape(size, ch), in_weights, gate_weights, out_weights)
     return result.reshape(rows, cols, ch)
 

time: 16.9 us -> 15.4 us (0.911)
  Pallas kernels: 15.4 us -> 14.6 us
  local copies, waits for them, and re-layouts: 1.3 us -> 0.6 us
    pallas_call x1, Pallas kernels: 15.4 us -> 14.6 us  [per_device(): pl.pallas_call(functools.partial(kernel, R, K, rows, cols), out_shape=jax...]
    unnamed x1, local copies, waits for them, and re-layouts: 1.3 us -> 0.6 us
where the time goes in v3:
time: 15.4 us; the launch traced here: 15.3 us
  Pallas kernels  14.6 us (95%)
  local copies, waits for them, and re-layouts  0.6 us (4%)
    pallas_call x1, Pallas kernels, per_device(): pl.pallas_call(functools.partial(kernel, R, K, rows, cols), out_shape=jax...  14.6 us
    unnamed x1, local copies, waits for them, and re-layouts  0.6 us

profile of v3, /device:TPU:1, one launch (start us, length us, event | category | flops | bytes accessed | tf_op | source)
XLA Modules:
  0.0 15.3 jit_solution(17730495502882455891)
XLA Ops:
  0.0 14.6 %shard_map.46 = bf16[32,128]{1,0:T(8,128)(2,1)S(1)} custom-call(bf16[32,128]{1,0:T(8,128)(2,1)} %bitcast.3, bf16[2,128,512]{2,1,0:T(8,128)(2,1)} %iw_hbm.1, bf16[2,128,128]{2,1,0:T(8,128)(2,1)} %gw_hbm.1, bf16[2,128,128]{2,1,0:T(8,128)(2,1)} %ow_hbm.1), custom_call_target="tpu_custom_call" | custom-call | tf_op jit(solution)/shard_map/pallas_call | solution.py:247
  14.7 0.6 %copy.6 = bf16[4,8,128]{2,1,0:T(8,128)(2,1)} copy(bf16[4,8,128]{2,1,0:T(8,128)(2,1)S(1)} %bitcast.2) | data formatting | bytes 16384
